TPU v7x, 256 devices: a whole 4x4x8 slice. The times are simulated.
256 devices in a mesh: section: 8 (over y, core), rows: 32 (over x, z).
Axes of the slice: x: 4, y: 4, z: 8, core: 2. Of those that a mesh axis runs over, the one named last changes fastest.
Arguments:
- grad_in: bfloat16 [8, 8192, 256], P('section', 'rows'), may hold values from -6 to 6
- grad_last: bfloat16 [8192, 256], P('rows'), may hold values from -6 to 6
- support: bfloat16 [8, 2, 2, 8192, 256], P('section', None, None, 'rows'), may hold values from -6 to 6
- preact: bfloat16 [8, 2, 2, 8192, 256], P('section', None, None, 'rows'), may hold values from -6 to 6
- weights: bfloat16 [8, 2, 256, 256], P('section'), may hold values from -0.375 to 0.375
- tile_vals: bfloat16 [8, 2, 3072, 128, 128], P('section', None, 'rows'), may hold values from -0.078125 to 0.078125
- tile_row: int32 [8, 2, 3072], P('section', None, 'rows'), may hold values from 0 to 1
- tile_col: int32 [8, 2, 3072], P('section', None, 'rows'), may hold values from 0 to 63, as said below
- tile_count: int32 [8, 2, 32], P('section', None, 'rows'), may hold values from 48 to 96, as said below
Outputs:
- handoff: bfloat16 [2, 8, 8192, 256], P(None, 'section', 'rows')
- init_grad: float32 [8, 2, 8192, 256], P('section', None, 'rows')
- weight_grad: float32 [8, 2, 256, 256], P('section')
Inputs may be any that keep to these rules, and one draw needn't show every extreme that they name: tile_count[s, t, d] is the number of live entries in device d's list; in every section and micro-batch some device has all 96 live. `tile_col`: for every section, micro-batch and pair of devices d and o with o != d, all entries of device d's list (live or padding) whose column tile lies in device o's rows name one and the same of o's 2 row tiles.
All inputs are finite; a program needn't handle non-finite values.
Results may differ from a plain program's by a relative error of at most 0.0066.
Values may be sent and summed in bfloat16 or wider, within the bound.
A program may use at most 128 MiB of HBM per device.

v0:
```python
import jax
import jax.numpy as jnp
from jax import lax
from jax.sharding import PartitionSpec as P

ALPHA = 0.1
BETA_SCALE = 0.5


def passed_along(block, axis, distance):
    devices = range(lax.axis_size(axis))
    route = [(i - distance, i) for i in devices if i - distance in devices]
    return lax.ppermute(block, axis, route)


def tile_product(gathered, values, row_local, index, count, row_tiles):
    tile = values.shape[-1]
    width = gathered.shape[-1]
    blocks = gathered.reshape(-1, tile, width)[index]
    products = jnp.einsum("kab,kbf->kaf", values, blocks, preferred_element_type=jnp.float32)
    live = jnp.arange(index.shape[0]) < count
    select = ((row_local[None, :] == jnp.arange(row_tiles)[:, None]) & live[None, :]).astype(
        jnp.float32
    )
    summed = jnp.einsum("ik,kaf->iaf", select, products, precision=lax.Precision.HIGHEST)
    return summed.reshape(row_tiles * tile, width)


def shards(grad_in, grad_last, support, preact, weights, tile_vals, tile_row, tile_col, tile_count):
    section = lax.axis_index("section")
    sections = lax.axis_size("section")
    ticks = support.shape[1]
    layers = support.shape[2]
    rows_dev, width = grad_last.shape
    tile = tile_vals.shape[-1]
    row_tiles = rows_dev // tile
    weight_acc = [jnp.zeros((width, width), jnp.float32) for layer in range(layers)]
    handed = []
    initial = []
    for tick in range(ticks):
        if tick == 0:
            grad = grad_in[0]
        else:
            passed = passed_along(handed[-1], "section", -1)
            grad = jnp.where(section == sections - 1, grad_last, passed)
        columns = tile_col[0, tick]
        count = tile_count[0, tick, 0]
        toward = jnp.zeros((rows_dev, width), jnp.float32)
        for layer in reversed(range(layers)):
            beta = jnp.log(BETA_SCALE / (layers * section + layer + 1).astype(jnp.float32) + 1.0)
            weight = weights[0, layer]
            masked = jnp.where(preact[0, tick, layer] > 0, grad, jnp.zeros_like(grad))
            term = beta * jnp.dot(
                support[0, tick, layer].T, masked, preferred_element_type=jnp.float32
            )
            weight_acc[layer] = weight_acc[layer] + lax.psum(term, "rows")
            image = (
                (1.0 - beta) * masked.astype(jnp.float32)
                + beta * jnp.dot(masked, weight.T, preferred_element_type=jnp.float32)
            ).astype(jnp.bfloat16)
            toward = toward + ALPHA * image.astype(jnp.float32)
            gathered = lax.all_gather(image, "rows", axis=0, tiled=True)
            spread = tile_product(
                gathered, tile_vals[0, tick], tile_row[0, tick], columns, count, row_tiles
            )
            grad = ((1.0 - ALPHA) * spread).astype(jnp.bfloat16)
        handed.append(grad)
        initial.append(toward)
    return (jnp.stack(handed)[:, None], jnp.stack(initial)[None], jnp.stack(weight_acc)[None])


def solution(mesh):
    return jax.shard_map(
        shards,
        mesh=mesh,
        in_specs=(
            P("section", "rows", None),
            P("rows", None),
            P("section", None, None, "rows", None),
            P("section", None, None, "rows", None),
            P("section", None, None, None),
            P("section", None, "rows", None, None),
            P("section", None, "rows"),
            P("section", None, "rows"),
            P("section", None, "rows"),
        ),
        out_specs=(
            P(None, "section", "rows", None),
            P("section", None, "rows", None),
            P("section", None, None, None),
        ),
        check_vma=False,
    )
```

profile of v0, /device:TPU:8, one launch (start us, length us, event | category | flops | bytes accessed | tf_op | source)
XLA Modules:
  0.0 648.4 jit_solution(17739819495514293798)
XLA Ops:
  7.2 0.0 all-gather.5.cloned.1.call-start
  7.3 2.1 fusion.15
  9.4 0.0 all-gather.5.cloned.1.call-update
  9.4 0.0 all-gather.7.cloned.1.call-start
  9.5 1.3 fusion.83
  10.8 0.6 iota_compare_fusion.1
  11.5 0.8 fusion.72
  12.3 0.8 slice_bitcast_fusion
  13.0 82.8 %all-gather.5.cloned.1.call-done = bf16[8192,256]{1,0:T(8,128)(2,1)} async-done(((bf16[256,256]{1,0:T(8,128)(2,1)}), bf16[8192,256]{1,0:T(8,128)(2,1)}) %all-gather.5.cloned.1.call-update) | async-done | bytes 4194320 | tf_op jit(solution)/shard_map/all_gather | solution.py:62
  95.8 8.1 %gather_fusion = bf16[96,128,256]{2,1,0:T(8,128)(2,1)} fusion(bf16[64,128,256]{2,1,0:T(8,128)(2,1)} %bitcast.141, s32[1024]{0:T(1024)S(1)} %pad_clamp_fusion.1), kind=kCustom, calls=%fused_computation | custom fusion | bytes 12583296 | tf_op jit(solution)/shard_map/gather | solution.py:19
  103.9 10.1 %convolution_bitcast_fusion.3 = f32[96,128,256]{1,2,0:T(8,128)} fusion(bf16[96,128,256]{2,1,0:T(8,128)(2,1)} %gather_fusion, bf16[1,2,96,128,128]{4,3,2,1,0:T(8,128)(2,1)} %param.14), kind=kOutput, calls=%fused_computation.7 | convolution fusion | flops 805306368 | bytes 22020096 | tf_op jit(solution)/shard_map/kab,kbf->kaf/dot_general | solution.py:20
  114.0 12.8 %copy.38 = f32[96,128,256]{2,0,1:T(8,128)} copy(f32[96,128,256]{1,2,0:T(8,128)} %convolution_bitcast_fusion.3) | data formatting | bytes 25165824 | tf_op jit(solution)/shard_map/kab,kbf->kaf/dot_general | solution.py:20
  126.7 0.0 copy-start
  126.7 0.0 copy-start.7
  126.7 7.1 %fusion.65 = f32[2,128,256]{2,0,1:T(2,128)S(1)} fusion(f32[96,128,256]{2,0,1:T(8,128)} %copy.38, pred[96]{0:T(512)(128)(4,1)S(1)} %iota_compare_fusion.1, s32[96]{0:T(128)S(1)} %get-tuple-element.18), kind=kOutput, calls=%fused_computation.97 | convolution fusion | flops 75497856 | bytes 12845536 | tf_op jit(solution)/shard_map/ik,kaf->iaf/dot_general | solution.py:25
  133.8 0.0 copy-done
  133.9 0.0 copy-done.7
  133.9 0.9 fusion.16
  134.8 0.0 all-gather.7.cloned.1.call-update
  134.8 0.2 all-gather.9.cloned.1.call-start
  135.0 78.9 %all-gather.7.cloned.1.call-done = bf16[8192,256]{1,0:T(8,128)(2,1)} async-done(((bf16[256,256]{1,0:T(8,128)(2,1)}), bf16[8192,256]{1,0:T(8,128)(2,1)}) %all-gather.7.cloned.1.call-update) | async-done | bytes 4194320 | tf_op jit(solution)/shard_map/all_gather | solution.py:62
  213.9 8.1 %gather_fusion.1 = bf16[96,128,256]{2,1,0:T(8,128)(2,1)} fusion(bf16[64,128,256]{2,1,0:T(8,128)(2,1)} %bitcast.144, s32[1024]{0:T(1024)S(1)} %pad_clamp_fusion.1), kind=kCustom, calls=%fused_computation.1 | custom fusion | bytes 12583296 | tf_op jit(solution)/shard_map/gather | solution.py:19
  222.0 10.1 %convolution_bitcast_fusion.2 = f32[96,128,256]{1,2,0:T(8,128)} fusion(bf16[96,128,256]{2,1,0:T(8,128)(2,1)} %gather_fusion.1, bf16[1,2,96,128,128]{4,3,2,1,0:T(8,128)(2,1)} %param.14), kind=kOutput, calls=%fused_computation.6 | convolution fusion | flops 805306368 | bytes 22020096 | tf_op jit(solution)/shard_map/kab,kbf->kaf/dot_general | solution.py:20
  232.1 12.8 %copy.41 = f32[96,128,256]{2,0,1:T(8,128)} copy(f32[96,128,256]{1,2,0:T(8,128)} %convolution_bitcast_fusion.2) | data formatting | bytes 25165824 | tf_op jit(solution)/shard_map/kab,kbf->kaf/dot_general | solution.py:20
  244.9 0.0 copy-start.5
  244.9 0.0 copy-start.1
  244.9 0.0 copy-start.6
  244.9 7.1 %fusion.63 = f32[2,128,256]{2,0,1:T(2,128)S(1)} fusion(f32[96,128,256]{2,0,1:T(8,128)} %copy.41, pred[96]{0:T(512)(128)(4,1)S(1)} %iota_compare_fusion.1, s32[96]{0:T(128)S(1)} %get-tuple-element.18), kind=kOutput, calls=%fused_computation.95 | convolution fusion | flops 75497856 | bytes 12845536 | tf_op jit(solution)/shard_map/ik,kaf->iaf/dot_general | solution.py:25
  252.0 1.9 collective-permute-start
  253.9 2.5 collective-permute-done
  256.4 0.0 copy-done.5
  256.4 0.9 add_convert_fusion
  257.3 0.0 all-gather.9.cloned.1.call-update
  257.3 0.3 all-reduce.3.cloned.1.call-start
  257.6 0.7 iota_compare_fusion
  258.3 0.0 copy-done.1
  258.3 0.0 copy-done.6
  258.3 0.2 fusion.24
  258.5 0.2 fusion.27
  258.8 0.9 fusion.9
  259.7 78.0 %all-gather.9.cloned.1.call-done = bf16[8192,256]{1,0:T(8,128)(2,1)} async-done(((bf16[256,256]{1,0:T(8,128)(2,1)}), bf16[8192,256]{1,0:T(8,128)(2,1)}) %all-gather.9.cloned.1.call-update) | async-done | bytes 4194320 | tf_op jit(solution)/shard_map/all_gather | solution.py:62
  337.7 8.1 %gather_fusion.2 = bf16[96,128,256]{2,1,0:T(8,128)(2,1)} fusion(bf16[64,128,256]{2,1,0:T(8,128)(2,1)} %bitcast.143, s32[1024]{0:T(1024)S(1)} %pad_clamp_fusion), kind=kCustom, calls=%fused_computation.2 | custom fusion | bytes 12583296 | tf_op jit(solution)/shard_map/gather | solution.py:19
  345.8 10.1 %convolution_bitcast_fusion.1 = f32[96,128,256]{1,2,0:T(8,128)} fusion(bf16[96,128,256]{2,1,0:T(8,128)(2,1)} %gather_fusion.2, bf16[1,2,96,128,128]{4,3,2,1,0:T(8,128)(2,1)} %param.14), kind=kOutput, calls=%fused_computation.5 | convolution fusion | flops 805306368 | bytes 22020096 | tf_op jit(solution)/shard_map/kab,kbf->kaf/dot_general | solution.py:20
  355.9 12.8 %copy.44 = f32[96,128,256]{2,0,1:T(8,128)} copy(f32[96,128,256]{1,2,0:T(8,128)} %convolution_bitcast_fusion.1) | data formatting | bytes 25165824 | tf_op jit(solution)/shard_map/kab,kbf->kaf/dot_general | solution.py:20
  368.6 7.0 %fusion.61 = f32[2,128,256]{2,0,1:T(2,128)S(1)} fusion(f32[96,128,256]{2,0,1:T(8,128)} %copy.44, pred[96]{0:T(512)(128)(4,1)S(1)} %iota_compare_fusion, s32[96]{0:T(128)S(1)} %get-tuple-element.17), kind=kOutput, calls=%fused_computation.93 | convolution fusion | flops 75497856 | bytes 12845536 | tf_op jit(solution)/shard_map/ik,kaf->iaf/dot_general | solution.py:25
  375.7 0.9 fusion.11
  376.7 0.0 all-reduce.3.cloned.1.call-update
  376.7 0.3 all-gather.11.cloned.1.call-start
  377.0 0.9 fusion.17
  377.9 0.0 all-gather.11.cloned.1.call-update
  377.9 0.0 copy-done.2
  377.9 0.0 copy-done.3
  378.0 0.0 copy-done.4
  378.0 0.9 multiply_bitcast_fusion
  378.9 0.8 maximum_bitcast_fusion
  379.8 141.9 %all-reduce.3.cloned.1.call-done = (f32[256,256]{0,1:T(8,128)}, f32[256,256]{0,1:T(8,128)}) async-done(((f32[256,256]{0,1:T(8,128)}, f32[256,256]{0,1:T(8,128)}), (f32[256,256]{0,1:T(8,128)}, f32[256,256]{0,1:T(8,128)})) %all-reduce.3.cloned.1.call-update) | async-done | bytes 524304 | tf_op jit(solution)/shard_map/psum | solution.py:56
  521.7 1.1 maximum_bitcast_fusion.1
  522.7 1.0 copy.50
  523.7 79.4 %all-gather.11.cloned.1.call-done = bf16[8192,256]{1,0:T(8,128)(2,1)} async-done(((bf16[256,256]{1,0:T(8,128)(2,1)}), bf16[8192,256]{1,0:T(8,128)(2,1)}) %all-gather.11.cloned.1.call-update) | async-done | bytes 4194320 | tf_op jit(solution)/shard_map/all_gather | solution.py:62
  603.1 8.1 %gather_fusion.3 = bf16[96,128,256]{2,1,0:T(8,128)(2,1)} fusion(bf16[64,128,256]{2,1,0:T(8,128)(2,1)} %bitcast.142, s32[1024]{0:T(1024)S(1)} %pad_clamp_fusion), kind=kCustom, calls=%fused_computation.3 | custom fusion | bytes 12583296 | tf_op jit(solution)/shard_map/gather | solution.py:19
  611.2 10.1 %convolution_bitcast_fusion = f32[96,128,256]{1,2,0:T(8,128)} fusion(bf16[96,128,256]{2,1,0:T(8,128)(2,1)} %gather_fusion.3, bf16[1,2,96,128,128]{4,3,2,1,0:T(8,128)(2,1)} %param.14), kind=kOutput, calls=%fused_computation.4 | convolution fusion | flops 805306368 | bytes 22020096 | tf_op jit(solution)/shard_map/kab,kbf->kaf/dot_general | solution.py:20
  621.3 12.8 %copy.47 = f32[96,128,256]{2,0,1:T(8,128)} copy(f32[96,128,256]{1,2,0:T(8,128)} %convolution_bitcast_fusion) | data formatting | bytes 25165824 | tf_op jit(solution)/shard_map/kab,kbf->kaf/dot_general | solution.py:20
  634.1 7.0 %fusion.59 = f32[2,128,256]{2,0,1:T(2,128)S(1)} fusion(f32[96,128,256]{2,0,1:T(8,128)} %copy.47, pred[96]{0:T(512)(128)(4,1)S(1)} %iota_compare_fusion, s32[96]{0:T(128)S(1)} %get-tuple-element.17), kind=kOutput, calls=%fused_computation.91 | convolution fusion | flops 75497856 | bytes 12845536 | tf_op jit(solution)/shard_map/ik,kaf->iaf/dot_general | solution.py:25
  641.1 0.7 maximum_bitcast_fusion.2
  (11 shorter events, 0.2 us)
Async XLA Ops:
  7.2 88.6 %all-gather.5.cloned.1.call-start = ((), (), s32[]{:S(2)}) async-start(), calls=%async_computation | async-start | bytes 4325376 | tf_op jit(solution)/shard_map/all_gather | solution.py:62
  9.4 204.6 %all-gather.7.cloned.1.call-start = ((), (), s32[]{:S(2)}) async-start(), calls=%async_computation.1 | async-start | bytes 4325376 | tf_op jit(solution)/shard_map/all_gather | solution.py:62
  126.7 7.1 %copy-start = (bf16[1,2,2,256,256]{4,3,2,1,0:T(8,128)(2,1)S(1)}, bf16[1,2,2,256,256]{4,3,2,1,0:T(8,128)(2,1)}, u32[]{:S(2)}) copy-start(bf16[1,2,2,256,256]{4,3,2,1,0:T(8,128)(2,1)} %param.12) | copy-start | bytes 1572868
  126.7 7.1 %copy-start.7 = (bf16[1,2,256,256]{3,2,1,0:T(8,128)(2,1)S(1)}, bf16[1,2,256,256]{3,2,1,0:T(8,128)(2,1)}, u32[]{:S(2)}) copy-start(bf16[1,2,256,256]{3,2,1,0:T(8,128)(2,1)} %param.13) | copy-start | bytes 786436
  134.8 202.9 %all-gather.9.cloned.1.call-start = ((), (), s32[]{:S(2)}) async-start(), calls=%async_computation.2 | async-start | bytes 4325376 | tf_op jit(solution)/shard_map/all_gather | solution.py:62
  244.9 11.6 %copy-start.5 = (bf16[256,256]{1,0:T(8,128)(2,1)S(1)}, bf16[256,256]{1,0:T(8,128)(2,1)}, u32[]{:S(2)}) copy-start(bf16[256,256]{1,0:T(8,128)(2,1)} %param.10) | copy-start | bytes 393220
  244.9 13.4 %copy-start.1 = (bf16[1,2,2,256,256]{4,3,2,1,0:T(8,128)(2,1)S(1)}, bf16[1,2,2,256,256]{4,3,2,1,0:T(8,128)(2,1)}, u32[]{:S(2)}) copy-start(bf16[1,2,2,256,256]{4,3,2,1,0:T(8,128)(2,1)} %param.11) | copy-start | bytes 1572868
  244.9 13.4 %copy-start.6 = (bf16[1,256,256]{2,1,0:T(8,128)(2,1)S(1)}, bf16[1,256,256]{2,1,0:T(8,128)(2,1)}, u32[]{:S(2)}) copy-start(bf16[1,256,256]{2,1,0:T(8,128)(2,1)} %param.9) | copy-start | bytes 393220
  252.0 4.4 collective-permute-start
  257.3 264.3 %all-reduce.3.cloned.1.call-start = ((), (), s32[]{:S(2)}) async-start(), calls=%async_computation.4 | async-start | bytes 1048576 | tf_op jit(solution)/shard_map/psum | solution.py:56
  368.6 9.3 %copy-start.2 = (bf16[256,256]{1,0:T(8,128)(2,1)S(1)}, bf16[256,256]{1,0:T(8,128)(2,1)}, u32[]{:S(2)}) copy-start(bf16[256,256]{1,0:T(8,128)(2,1)} %fusion.15) | copy-start | bytes 393220
  368.6 9.3 %copy-start.3 = (bf16[256,256]{1,0:T(8,128)(2,1)S(1)}, bf16[256,256]{1,0:T(8,128)(2,1)}, u32[]{:S(2)}) copy-start(bf16[256,256]{1,0:T(8,128)(2,1)} %fusion.16) | copy-start | bytes 393220
  368.6 9.3 %copy-start.4 = (bf16[256,256]{1,0:T(8,128)(2,1)S(1)}, bf16[256,256]{1,0:T(8,128)(2,1)}, u32[]{:S(2)}) copy-start(bf16[256,256]{1,0:T(8,128)(2,1)} %add_convert_fusion) | copy-start | bytes 393220
  376.7 226.5 %all-gather.11.cloned.1.call-start = ((), (), s32[]{:S(2)}) async-start(), calls=%async_computation.3 | async-start | bytes 4325376 | tf_op jit(solution)/shard_map/all_gather | solution.py:62
Sparse Core Ops, SparseCore 0:
  11.2 84.5 all-gather.4
  134.9 78.9 all-gather.6
  257.5 80.1 all-gather.8
  376.8 144.8 all-reduce.2
  524.5 78.6 all-gather.10
where the time goes:
time: 649 us; the launch traced here: 648 us
  waiting for transfers between devices  464 us (71%)
  local copies, waits for them, and re-layouts  86.5 us (13%)
  matrix products  75.5 us (12%)
  between operations  14.2 us (2%)
    all_gather x4, waiting for transfers between devices, shards(): gathered = lax.all_gather(image, 'rows', axis=0, tiled=True)  319 us
    psum x1, waiting for transfers between devices, shards(): weight_acc[layer] = weight_acc[layer] + lax.psum(term, 'rows')  142 us
    dot_general x4, local copies, waits for them, and re-layouts, tile_product(): jnp.einsum('kab,kbf->kaf', values, blocks, preferred_element_type=jnp.flo...  51 us
    dot_general x4, matrix products, tile_product(): jnp.einsum('kab,kbf->kaf', values, blocks, preferred_element_type=jnp.flo...  40.3 us
    gather x4, local copies, waits for them, and re-layouts, tile_product(): blocks = gathered.reshape(-1, tile, width)[index]  32.4 us
    dot_general x4, matrix products, tile_product(): jnp.einsum('ik,kaf->iaf', select, products, precision=lax.Precision.HIGHEST)  28.2 us
  transfers between devices with their start and end apart: 6, of which 6 were waited for; matrix products, arithmetic and copies ran while one was open for 2% of the time, Pallas kernels for 0%

commit v1 on v0

--- a/solution.py
+++ b/solution.py
@@ -2,9 +2,11 @@
 import jax.numpy as jnp
 from jax import lax
 from jax.sharding import PartitionSpec as P
+from jax.lax import all_gather
 
 ALPHA = 0.1
 BETA_SCALE = 0.5
+signs_begin = lambda original: jnp.sum(all_gather(original, "rows"), 0)
 
 
 def passed_along(block, axis, distance):
@@ -53,7 +55,7 @@
             term = beta * jnp.dot(
                 support[0, tick, layer].T, masked, preferred_element_type=jnp.float32
             )
-            weight_acc[layer] = weight_acc[layer] + lax.psum(term, "rows")
+            weight_acc[layer] = weight_acc[layer] + signs_begin(term)
             image = (
                 (1.0 - beta) * masked.astype(jnp.float32)
                 + beta * jnp.dot(masked, weight.T, preferred_element_type=jnp.float32)

time: 649 us -> 864 us (1.33)
  waiting for transfers between devices: 464 us -> 626 us
  local copies, waits for them, and re-layouts: 86.5 us -> 121 us
  other arithmetic: 5.81 us -> 18 us
    all_gather x0 -> x4, waiting for transfers between devices: none -> 314 us  [signs_begin = lambda original: jnp.sum(all_gather(original, 'rows'), 0)]
    psum x1 -> x0, waiting for transfers between devices: 142 us -> none  [shards(): weight_acc[layer] = weight_acc[layer] + lax.psum(term, 'rows')]
    unnamed x17 -> x25, local copies, waits for them, and re-layouts: 1.03 us -> 35.1 us
    reduce_sum x0 -> x2, other arithmetic: none -> 14.1 us  [signs_begin = lambda original: jnp.sum(all_gather(original, 'rows'), 0)]
    all_gather x4, waiting for transfers between devices: 319 us -> 310 us  [shards(): gathered = lax.all_gather(image, 'rows', axis=0, tiled=True)]
  transfers between devices with their start and end apart: 6 -> 9, of which waited for: 6 -> 9; matrix products, arithmetic and copies ran while one was open for 2% -> 14% of each run, Pallas kernels for 0% -> 0%
where the time goes in v1:
time: 864 us; the launch traced here: 857 us
  waiting for transfers between devices  626 us (72%)
  local copies, waits for them, and re-layouts  121 us (14%)
  matrix products  74.1 us (9%)
  other arithmetic  18 us (2%)
  between operations  14.7 us (2%)
    all_gather x4, waiting for transfers between devices, signs_begin = lambda original: jnp.sum(all_gather(original, 'rows'), 0)  314 us
    all_gather x4, waiting for transfers between devices, shards(): gathered = lax.all_gather(image, 'rows', axis=0, tiled=True)  310 us
    dot_general x4, local copies, waits for them, and re-layouts, tile_product(): jnp.einsum('kab,kbf->kaf', values, blocks, preferred_element_type=jnp.flo...  51.3 us
    dot_general x4, matrix products, tile_product(): jnp.einsum('kab,kbf->kaf', values, blocks, preferred_element_type=jnp.flo...  40.3 us
    unnamed x25, local copies, waits for them, and re-layouts  35.1 us
    gather x4, local copies, waits for them, and re-layouts, tile_product(): blocks = gathered.reshape(-1, tile, width)[index]  32.9 us
    dot_general x4, matrix products, tile_product(): jnp.einsum('ik,kaf->iaf', select, products, precision=lax.Precision.HIGHEST)  25.4 us
  transfers between devices with their start and end apart: 9, of which 9 were waited for; matrix products, arithmetic and copies ran while one was open for 14% of the time, Pallas kernels for 0%

profile of v1, /device:TPU:8, one launch (start us, length us, event | category | flops | bytes accessed | tf_op | source)
XLA Modules:
  0.0 857.4 jit_solution(2083172210814501196)
XLA Ops:
  7.2 0.0 all-gather.13.cloned.1.call-start
  7.3 2.1 fusion.15
  9.4 0.0 all-gather.13.cloned.1.call-update
  9.4 0.0 all-gather.15.cloned.1.call-start
  9.5 1.3 fusion.81
  10.8 0.6 iota_compare_fusion.1
  11.5 0.8 fusion.70
  12.3 0.8 slice_bitcast_fusion
  13.0 82.2 %all-gather.13.cloned.1.call-done = bf16[8192,256]{1,0:T(8,128)(2,1)} async-done(((bf16[256,256]{1,0:T(8,128)(2,1)}), bf16[8192,256]{1,0:T(8,128)(2,1)}) %all-gather.13.cloned.1.call-update) | async-done | bytes 4194320 | tf_op jit(solution)/shard_map/all_gather | solution.py:64
  95.2 8.1 gather_fusion
  103.4 10.1 %convolution_bitcast_fusion.3 = f32[96,128,256]{1,2,0:T(8,128)} fusion(bf16[96,128,256]{2,1,0:T(8,128)(2,1)} %gather_fusion, bf16[1,2,96,128,128]{4,3,2,1,0:T(8,128)(2,1)} %param.14), kind=kOutput, calls=%fused_computation.11 | convolution fusion | flops 805306368 | bytes 22020096 | tf_op jit(solution)/shard_map/kab,kbf->kaf/dot_general | solution.py:22
  113.4 12.8 %copy.56 = f32[96,128,256]{2,0,1:T(8,128)} copy(f32[96,128,256]{1,2,0:T(8,128)} %convolution_bitcast_fusion.3) | data formatting | bytes 25165824 | tf_op jit(solution)/shard_map/kab,kbf->kaf/dot_general | solution.py:22
  126.2 7.1 fusion.63
  133.4 0.9 fusion.16
  134.2 0.0 all-gather.15.cloned.1.call-update
  134.3 0.2 all-gather.17.cloned.1.call-start
  134.5 78.9 %all-gather.15.cloned.1.call-done = bf16[8192,256]{1,0:T(8,128)(2,1)} async-done(((bf16[256,256]{1,0:T(8,128)(2,1)}), bf16[8192,256]{1,0:T(8,128)(2,1)}) %all-gather.15.cloned.1.call-update) | async-done | bytes 4194320 | tf_op jit(solution)/shard_map/all_gather | solution.py:64
  213.4 8.1 gather_fusion.1
  221.6 10.1 %convolution_bitcast_fusion.2 = f32[96,128,256]{1,2,0:T(8,128)} fusion(bf16[96,128,256]{2,1,0:T(8,128)(2,1)} %gather_fusion.1, bf16[1,2,96,128,128]{4,3,2,1,0:T(8,128)(2,1)} %param.14), kind=kOutput, calls=%fused_computation.10 | convolution fusion | flops 805306368 | bytes 22020096 | tf_op jit(solution)/shard_map/kab,kbf->kaf/dot_general | solution.py:22
  231.6 12.8 %copy.59 = f32[96,128,256]{2,0,1:T(8,128)} copy(f32[96,128,256]{1,2,0:T(8,128)} %convolution_bitcast_fusion.2) | data formatting | bytes 25165824 | tf_op jit(solution)/shard_map/kab,kbf->kaf/dot_general | solution.py:22
  244.4 7.1 fusion.61
  251.6 1.9 collective-permute-start
  253.5 2.5 collective-permute-done
  256.0 0.9 add_convert_fusion
  256.9 0.0 all-gather.17.cloned.1.call-update
  256.9 0.0 all-gather.25.cloned.1.call-start
  257.0 0.9 fusion.9
  258.0 0.0 all-gather.25.cloned.1.call-update
  258.0 0.0 all-gather.21.cloned.1.call-start
  258.0 0.9 fusion.11
  259.0 0.0 all-gather.21.cloned.1.call-update
  259.0 0.3 all-gather.19.cloned.1.call-start
  259.2 0.7 iota_compare_fusion
  259.9 77.4 %all-gather.17.cloned.1.call-done = bf16[8192,256]{1,0:T(8,128)(2,1)} async-done(((bf16[256,256]{1,0:T(8,128)(2,1)}), bf16[8192,256]{1,0:T(8,128)(2,1)}) %all-gather.17.cloned.1.call-update) | async-done | bytes 4194320 | tf_op jit(solution)/shard_map/all_gather | solution.py:64
  337.3 8.1 gather_fusion.2
  345.4 10.1 %convolution_bitcast_fusion.1 = f32[96,128,256]{1,2,0:T(8,128)} fusion(bf16[96,128,256]{2,1,0:T(8,128)(2,1)} %gather_fusion.2, bf16[1,2,96,128,128]{4,3,2,1,0:T(8,128)(2,1)} %param.14), kind=kOutput, calls=%fused_computation.9 | convolution fusion | flops 805306368 | bytes 22020096 | tf_op jit(solution)/shard_map/kab,kbf->kaf/dot_general | solution.py:22
  355.5 12.9 %copy.62 = f32[96,128,256]{2,0,1:T(8,128)} copy(f32[96,128,256]{1,2,0:T(8,128)} %convolution_bitcast_fusion.1) | data formatting | bytes 25165824 | tf_op jit(solution)/shard_map/kab,kbf->kaf/dot_general | solution.py:22
  368.3 7.1 fusion.59
  375.4 0.9 fusion.17
  376.3 0.0 all-gather.19.cloned.1.call-update
  376.4 0.0 all-gather.27.cloned.1.call-start
  376.4 0.9 fusion.8
  377.3 0.0 all-gather.27.cloned.1.call-update
  377.4 0.3 all-gather.23.cloned.1.call-start
  377.7 0.9 fusion.10
  378.6 0.0 all-gather.23.cloned.1.call-update
  378.7 62.4 %all-gather.25.cloned.1.call-done = f32[8192,256]{0,1:T(8,128)} async-done(((f32[256,256]{0,1:T(8,128)}), f32[8192,256]{0,1:T(8,128)}) %all-gather.25.cloned.1.call-update) | async-done | bytes 8388624 | tf_op jit(solution)/shard_map/all_gather | solution.py:9
  441.1 10.1 %copy.75 = f32[32,8,32,256]{3,2,1,0:T(8,128)} copy(f32[32,8,32,256]{3,1,2,0:T(8,128)} %bitcast.171) | data formatting | bytes 16777216
  451.2 94.4 %all-gather.21.cloned.1.call-done = f32[8192,256]{0,1:T(8,128)} async-done(((f32[256,256]{0,1:T(8,128)}), f32[8192,256]{0,1:T(8,128)}) %all-gather.21.cloned.1.call-update) | async-done | bytes 8388624 | tf_op jit(solution)/shard_map/all_gather | solution.py:9
  545.5 10.1 %copy.73 = f32[32,8,32,256]{3,2,1,0:T(8,128)} copy(f32[32,8,32,256]{3,1,2,0:T(8,128)} %bitcast.172) | data formatting | bytes 16777216
  555.7 0.8 maximum_bitcast_fusion
  556.5 71.1 %all-gather.19.cloned.1.call-done = bf16[8192,256]{1,0:T(8,128)(2,1)} async-done(((bf16[256,256]{1,0:T(8,128)(2,1)}), bf16[8192,256]{1,0:T(8,128)(2,1)}) %all-gather.19.cloned.1.call-update) | async-done | bytes 4194320 | tf_op jit(solution)/shard_map/all_gather | solution.py:64
  627.6 8.6 %gather_fusion.3 = bf16[96,128,256]{2,1,0:T(8,128)(2,1)} fusion(bf16[64,128,256]{2,1,0:T(8,128)(2,1)} %bitcast.167, s32[1024]{0:T(1024)S(1)} %pad_clamp_fusion), kind=kCustom, calls=%fused_computation.3 | custom fusion | bytes 12583296 | tf_op jit(solution)/shard_map/gather | solution.py:21
  636.2 10.1 %convolution_bitcast_fusion = f32[96,128,256]{1,2,0:T(8,128)} fusion(bf16[96,128,256]{2,1,0:T(8,128)(2,1)} %gather_fusion.3, bf16[1,2,96,128,128]{4,3,2,1,0:T(8,128)(2,1)} %param.14), kind=kOutput, calls=%fused_computation.8 | convolution fusion | flops 805306368 | bytes 22020096 | tf_op jit(solution)/shard_map/kab,kbf->kaf/dot_general | solution.py:22
  646.3 12.9 %copy.65 = f32[96,128,256]{2,0,1:T(8,128)} copy(f32[96,128,256]{1,2,0:T(8,128)} %convolution_bitcast_fusion) | data formatting | bytes 25165824 | tf_op jit(solution)/shard_map/kab,kbf->kaf/dot_general | solution.py:22
  659.1 72.4 %all-gather.27.cloned.1.call-done = f32[8192,256]{0,1:T(8,128)} async-done(((f32[256,256]{0,1:T(8,128)}), f32[8192,256]{0,1:T(8,128)}) %all-gather.27.cloned.1.call-update) | async-done | bytes 8388624 | tf_op jit(solution)/shard_map/all_gather | solution.py:9
  731.6 7.1 copy.76
  738.7 4.2 fusion.57
  742.9 0.7 maximum_bitcast_fusion.2
  743.6 7.2 bitcast_reduce_fusion
  750.8 84.7 %all-gather.23.cloned.1.call-done = f32[8192,256]{0,1:T(8,128)} async-done(((f32[256,256]{0,1:T(8,128)}), f32[8192,256]{0,1:T(8,128)}) %all-gather.23.cloned.1.call-update) | async-done | bytes 8388624 | tf_op jit(solution)/shard_map/all_gather | solution.py:9
  835.6 6.8 copy.74
  842.4 6.9 bitcast_reduce_fusion.2
  849.4 1.0 copy.68
  (32 shorter events, 0.4 us)
Async XLA Ops:
  7.2 88.1 %all-gather.13.cloned.1.call-start = ((), (), s32[]{:S(2)}) async-start(), calls=%async_computation | async-start | bytes 4325376 | tf_op jit(solution)/shard_map/all_gather | solution.py:64
  9.4 204.0 %all-gather.15.cloned.1.call-start = ((), (), s32[]{:S(2)}) async-start(), calls=%async_computation.1 | async-start | bytes 4325376 | tf_op jit(solution)/shard_map/all_gather | solution.py:64
  126.2 7.1 copy-start.6
  126.2 7.1 copy-start.8
  134.3 203.0 %all-gather.17.cloned.1.call-start = ((), (), s32[]{:S(2)}) async-start(), calls=%async_computation.2 | async-start | bytes 4325376 | tf_op jit(solution)/shard_map/all_gather | solution.py:64
  244.4 11.6 %copy-start.5 = (bf16[256,256]{1,0:T(8,128)(2,1)S(1)}, bf16[256,256]{1,0:T(8,128)(2,1)}, u32[]{:S(2)}) copy-start(bf16[256,256]{1,0:T(8,128)(2,1)} %param.10) | copy-start | bytes 393220
  244.4 12.6 %copy-start.7 = (bf16[1,2,2,256,256]{4,3,2,1,0:T(8,128)(2,1)S(1)}, bf16[1,2,2,256,256]{4,3,2,1,0:T(8,128)(2,1)}, u32[]{:S(2)}) copy-start(bf16[1,2,2,256,256]{4,3,2,1,0:T(8,128)(2,1)} %param.11) | copy-start | bytes 1572868
  244.4 12.6 %copy-start.9 = (bf16[1,256,256]{2,1,0:T(8,128)(2,1)S(1)}, bf16[1,256,256]{2,1,0:T(8,128)(2,1)}, u32[]{:S(2)}) copy-start(bf16[1,256,256]{2,1,0:T(8,128)(2,1)} %param.9) | copy-start | bytes 393220
  251.6 4.4 collective-permute-start
  256.9 184.2 %all-gather.25.cloned.1.call-start = ((), (), s32[]{:S(2)}) async-start(), calls=%async_computation.6 | async-start | bytes 8650752 | tf_op jit(solution)/shard_map/all_gather | solution.py:9
  258.0 287.6 %all-gather.21.cloned.1.call-start = ((), (), s32[]{:S(2)}) async-start(), calls=%async_computation.4 | async-start | bytes 8650752 | tf_op jit(solution)/shard_map/all_gather | solution.py:9
  259.0 368.6 %all-gather.19.cloned.1.call-start = ((), (), s32[]{:S(2)}) async-start(), calls=%async_computation.3 | async-start | bytes 4325376 | tf_op jit(solution)/shard_map/all_gather | solution.py:64
  368.3 10.3 %copy-start.1 = (bf16[256,256]{1,0:T(8,128)(2,1)S(1)}, bf16[256,256]{1,0:T(8,128)(2,1)}, u32[]{:S(2)}) copy-start(bf16[256,256]{1,0:T(8,128)(2,1)} %fusion.15) | copy-start | bytes 393220
  368.3 10.3 %copy-start.2 = (bf16[256,256]{1,0:T(8,128)(2,1)S(1)}, bf16[256,256]{1,0:T(8,128)(2,1)}, u32[]{:S(2)}) copy-start(bf16[256,256]{1,0:T(8,128)(2,1)} %fusion.16) | copy-start | bytes 393220
  376.4 355.2 %all-gather.27.cloned.1.call-start = ((), (), s32[]{:S(2)}) async-start(), calls=%async_computation.7 | async-start | bytes 8650752 | tf_op jit(solution)/shard_map/all_gather | solution.py:9
  377.4 458.2 %all-gather.23.cloned.1.call-start = ((), (), s32[]{:S(2)}) async-start(), calls=%async_computation.5 | async-start | bytes 8650752 | tf_op jit(solution)/shard_map/all_gather | solution.py:9
  545.5 10.1 %copy-start.3 = (bf16[256,256]{1,0:T(8,128)(2,1)S(1)}, bf16[256,256]{1,0:T(8,128)(2,1)}, u32[]{:S(2)}) copy-start(bf16[256,256]{1,0:T(8,128)(2,1)} %add_convert_fusion) | copy-start | bytes 393220
  545.5 10.1 %copy-start.4 = (bf16[256,256]{1,0:T(8,128)(2,1)S(1)}, bf16[256,256]{1,0:T(8,128)(2,1)}, u32[]{:S(2)}) copy-start(bf16[256,256]{1,0:T(8,128)(2,1)} %fusion.17) | copy-start | bytes 393220
  731.6 7.1 copy-start
Sparse Core Ops, SparseCore 0:
  10.6 84.5 all-gather.12
  134.4 78.9 all-gather.14
  257.1 80.1 all-gather.16
  340.2 100.8 all-gather.24
  444.0 101.4 all-gather.20
  548.0 79.5 all-gather.18
  630.6 100.8 all-gather.26
  734.0 101.4 all-gather.22
